TPU v7x, 512 devices: a whole 4x8x8 slice. The times are simulated.
512 devices in a mesh: patch: 2 (over core), lat: 8 (over y), lon: 32 (over z, x).
Axes of the slice: x: 4, y: 8, z: 8, core: 2. Of those that a mesh axis runs over, the one named last changes fastest.
Arguments:
- velocity: float32 [2, 3, 128, 256, 128], P('patch', None, 'lat', 'lon'), may hold values from -6 to 6
- forcing: float32 [2, 3, 128, 256, 128], P('patch', None, 'lat', 'lon'), may hold values from -3 to 3
- viscosity: float32 [2, 128, 256, 128], P('patch', 'lat', 'lon'), may hold values from 1 to 10
- ghost_slots: int32 [2, 768], P('patch'), may hold values from 0 to 767, each once within a row
- corner_rows: int32 [2, 8, 96], P('patch', 'lat', 'lon'), may hold values from 0 to 15
- corner_cols: int32 [2, 8, 96], P('patch', 'lat', 'lon'), may hold values from 0 to 7
- corner_weights: float32 [2, 8, 4, 96], P('patch', 'lat', None, 'lon'), may hold values from 0 to 1, as said below
Outputs:
- new_velocity: float32 [2, 3, 128, 256, 128], P('patch', None, 'lat', 'lon')
- residual: float32 [2, 3, 128, 256, 128], P('patch', None, 'lat', 'lon')
Inputs may be any that keep to these rules, and one draw needn't show every extreme that they name: `ghost_slots`: each row names every slot of the other patch exactly once. `corner_rows`: the row below the corner is read too, from the next device or as zero beyond the patch. `corner_cols`: the column after the corner is read too, from the next device or as zero beyond the patch. `corner_weights`: the four weights of a slot are (1 - s)(1 - t), s(1 - t), (1 - s)t and st for some s and t in [0, 1).
All inputs are finite; a program needn't handle non-finite values.
Results may differ from a plain program's by a relative error of at most 0.0001.
Values sent between devices are 32-bit elements; how exact they have to be, the bound alone decides.
No kernel may reach another device: no remote copies, remote signals or barrier semaphores. Data moves between devices by JAX's collectives and lax.ppermute only.
A program may use at most 64 MiB of HBM per device.

v0:
```python
import jax
import jax.numpy as jnp
from jax import lax
from jax.sharding import PartitionSpec as P

SWEEPS = 2
COARSE = 8
RELAX = 0.8


def with_halo(shard, sides, width):
    for axis, dim in sides:
        devices, length = (lax.axis_size(axis), shard.shape[dim])
        up = [(i, (i + 1) % devices) for i in range(devices - 1)]
        down = [(j, i) for i, j in up]
        last = lax.slice_in_dim(shard, length - width, length, axis=dim)
        first = lax.slice_in_dim(shard, 0, width, axis=dim)
        before = lax.ppermute(last, axis, up)
        after = lax.ppermute(first, axis, down)
        shard = jnp.concatenate([before, shard, after], axis=dim)
    return shard


def swapped(value, axis, apart):
    mask = 2**apart
    pairs = [(source, source ^ mask) for source in range(lax.axis_size(axis))]
    return lax.ppermute(value, axis, pairs)


def face_terms(padded_visc, weight_scale):
    centre = padded_visc[1:-1, 1:-1, 1:-1]
    return (
        weight_scale * (centre + padded_visc[:-2, 1:-1, 1:-1]),
        weight_scale * (centre + padded_visc[2:, 1:-1, 1:-1]),
        weight_scale * (centre + padded_visc[1:-1, :-2, 1:-1]),
        weight_scale * (centre + padded_visc[1:-1, 2:, 1:-1]),
        weight_scale * (centre + padded_visc[1:-1, 1:-1, :-2]),
        weight_scale * (centre + padded_visc[1:-1, 1:-1, 2:]),
    )


def diagonal_of(face_coefs):
    return (
        face_coefs[0]
        + face_coefs[1]
        + face_coefs[2]
        + face_coefs[3]
        + face_coefs[4]
        + face_coefs[5]
    )


def neighbour_sum(padded, face_coefs):
    summed = face_coefs[0] * padded[:, :-2, 1:-1, 1:-1]
    summed = summed + face_coefs[1] * padded[:, 2:, 1:-1, 1:-1]
    summed = summed + face_coefs[2] * padded[:, 1:-1, :-2, 1:-1]
    summed = summed + face_coefs[3] * padded[:, 1:-1, 2:, 1:-1]
    summed = summed + face_coefs[4] * padded[:, 1:-1, 1:-1, :-2]
    summed = summed + face_coefs[5] * padded[:, 1:-1, 1:-1, 2:]
    return summed


def bilinear(weight_rows, corner_list):
    summed = weight_rows[0][None, :, None] * corner_list[0]
    summed = summed + weight_rows[1][None, :, None] * corner_list[1]
    summed = summed + weight_rows[2][None, :, None] * corner_list[2]
    summed = summed + weight_rows[3][None, :, None] * corner_list[3]
    return summed


def clamp_take(source_array, along_dim, offset, block_size, whole_size, margin):
    position = offset + jnp.arange(-margin, block_size + margin, dtype=jnp.int32)
    picked = jnp.clip(position, 0, whole_size - 1) - offset + margin
    return jnp.take(source_array, picked, axis=along_dim)


def per_device(velocity, forcing, viscosity, ghost_slots, corner_rows, corner_cols, corner_weights):
    start_field = velocity[0]
    force_block = forcing[0]
    viscous = viscosity[0]
    row_block, col_block, levels = viscous.shape
    lat_count = lax.axis_size("lat")
    lon_count = lax.axis_size("lon")
    lat_index = lax.axis_index("lat")
    lon_index = lax.axis_index("lon")
    lat_cells = row_block * lat_count
    lon_cells = col_block * lon_count
    row_offset = lat_index * row_block
    col_offset = lon_index * col_block
    ghost_count = ghost_slots.shape[1]
    order_row = ghost_slots[0]
    rim_width = 1
    visc_rim = with_halo(viscous, (("lat", 0), ("lon", 1)), 2)
    visc_ext = clamp_take(visc_rim, 0, row_offset, row_block, lat_cells, 2)
    visc_ext = clamp_take(visc_ext, 1, col_offset, col_block, lon_cells, 2)
    visc_ext = jnp.pad(visc_ext, ((0, 0), (0, 0), (2, 2)), mode="edge")
    loop_coefs = face_terms(visc_ext[:, :, 1:-1], 0.5)
    loop_diag = diagonal_of(loop_coefs)
    loop_rows = row_offset + jnp.arange(-1, row_block + 1, dtype=jnp.int32)
    loop_cols = col_offset + jnp.arange(-1, col_block + 1, dtype=jnp.int32)
    loop_parity = (
        loop_rows[:, None, None]
        + loop_cols[None, :, None]
        + jnp.arange(levels, dtype=jnp.int32)[None, None, :]
    ) % 2
    loop_inside = (
        ((loop_rows >= 0) & (loop_rows < lat_cells))[:, None]
        & ((loop_cols >= 0) & (loop_cols < lon_cells))[None, :]
    )[:, :, None]
    ext_rows = row_offset + jnp.arange(-rim_width, row_block + rim_width, dtype=jnp.int32)
    ext_cols = col_offset + jnp.arange(-rim_width, col_block + rim_width, dtype=jnp.int32)
    rows_inside = (ext_rows >= 0) & (ext_rows < lat_cells)
    cols_inside = (ext_cols >= 0) & (ext_cols < lon_cells)

    def slot_lookup(ghost_ids):
        return jnp.take(order_row, jnp.clip(ghost_ids, 0, ghost_count - 1))

    rim_slots = (
        slot_lookup(ext_cols),
        slot_lookup(lon_cells + ext_cols),
        slot_lookup(2 * lon_cells + ext_rows),
        slot_lookup(2 * lon_cells + lat_cells + ext_rows),
    )

    def extend(block_field):
        return with_halo(block_field, (("lat", 1), ("lon", 2)), rim_width)

    grown_field = extend(start_field)
    source_view = grown_field[
        :, rim_width : rim_width + row_block + 1, rim_width : rim_width + col_block + 1
    ]
    rows_given = corner_rows[0, 0]
    cols_given = corner_cols[0, 0]
    weights = corner_weights[0, 0]
    corners = (
        source_view[:, rows_given, cols_given],
        source_view[:, rows_given + 1, cols_given],
        source_view[:, rows_given, cols_given + 1],
        source_view[:, rows_given + 1, cols_given + 1],
    )
    corner_slots = jnp.transpose(jnp.stack(corners, axis=0), (2, 0, 1, 3))
    weight_slots = jnp.transpose(weights)
    partner_corners, partner_weights = swapped((corner_slots, weight_slots), "patch", 0)
    blank_rims = tuple(
        (jnp.zeros((3, rim_slot.shape[0], levels), jnp.float32) for rim_slot in rim_slots)
    )
    piece_corners = lax.all_gather(partner_corners, ("lat", "lon"), axis=0, tiled=True)
    piece_weights = lax.all_gather(partner_weights, ("lat", "lon"), axis=0, tiled=True)
    count_here = piece_corners.shape[0]
    outcome = []
    for rim_index in range(4):
        local_ids = rim_slots[rim_index]
        inside = (local_ids >= 0) & (local_ids < count_here)
        safe_ids = jnp.clip(local_ids, 0, count_here - 1)
        got_corners = jnp.transpose(jnp.take(piece_corners, safe_ids, axis=0), (1, 2, 0, 3))
        got_weights = jnp.transpose(jnp.take(piece_weights, safe_ids, axis=0))
        ghost_value = bilinear(
            got_weights, (got_corners[0], got_corners[1], got_corners[2], got_corners[3])
        )
        outcome.append(jnp.where(inside[None, :, None], ghost_value, blank_rims[rim_index]))
    rim_values = tuple(outcome)
    top_valid = cols_inside & (lat_index == 0)
    bottom_valid = cols_inside & (lat_index == lat_count - 1)
    left_valid = rows_inside & (lon_index == 0)
    right_valid = rows_inside & (lon_index == lon_count - 1)
    lower_row = rim_width + row_block
    right_col = rim_width + col_block

    def with_ghosts(grown):
        grown = grown.at[:, rim_width - 1].set(
            jnp.where(top_valid[None, :, None], rim_values[0], grown[:, rim_width - 1])
        )
        grown = grown.at[:, lower_row].set(
            jnp.where(bottom_valid[None, :, None], rim_values[1], grown[:, lower_row])
        )
        grown = grown.at[:, :, rim_width - 1].set(
            jnp.where(left_valid[None, :, None], rim_values[2], grown[:, :, rim_width - 1])
        )
        grown = grown.at[:, :, right_col].set(
            jnp.where(right_valid[None, :, None], rim_values[3], grown[:, :, right_col])
        )
        return grown

    def relax_colour(grown, colour, margin):
        first_cell = rim_width - margin
        row_end = rim_width + row_block + margin
        col_end = rim_width + col_block + margin
        loop_shift = 1 - margin
        region_rows = row_block + 2 * margin
        region_cols = col_block + 2 * margin
        padded = jnp.pad(grown, ((0, 0), (0, 0), (0, 0), (1, 1)))
        region_coefs = tuple(
            (
                face_coef[
                    loop_shift : loop_shift + region_rows, loop_shift : loop_shift + region_cols
                ]
                for face_coef in loop_coefs
            )
        )
        region_diag = loop_diag[
            loop_shift : loop_shift + region_rows, loop_shift : loop_shift + region_cols
        ]
        relaxed = (force_block + neighbour_sum(padded, region_coefs)) / region_diag
        chosen = (
            loop_parity[
                loop_shift : loop_shift + region_rows, loop_shift : loop_shift + region_cols
            ]
            == colour
        ) & loop_inside[
            loop_shift : loop_shift + region_rows, loop_shift : loop_shift + region_cols
        ]
        updated = jnp.where(chosen[None], relaxed, grown[:, first_cell:row_end, first_cell:col_end])
        return grown.at[:, first_cell:row_end, first_cell:col_end].set(updated)

    def interior(grown):
        return grown[:, rim_width : rim_width + row_block, rim_width : rim_width + col_block]

    current = with_ghosts(grown_field)
    for sweep_index in range(SWEEPS):
        if sweep_index > 0:
            current = with_ghosts(extend(interior(current)))
        current = relax_colour(current, 0, 0)
        current = with_ghosts(extend(interior(current)))
        current = relax_colour(current, 1, 0)
    smoothed = interior(current)
    grown_last = with_ghosts(extend(smoothed))
    padded_last = jnp.pad(grown_last, ((0, 0), (0, 0), (0, 0), (1, 1)))
    inner_coefs = tuple((face_coef[1:-1, 1:-1] for face_coef in loop_coefs))
    inner_diag = loop_diag[1:-1, 1:-1]
    residual_field = force_block - (inner_diag * smoothed - neighbour_sum(padded_last, inner_coefs))
    half_rows = row_block // 2
    half_cols = col_block // 2
    half_levels = levels // 2
    coarse_rhs = residual_field.reshape(3, half_rows, 2, half_cols, 2, half_levels, 2).mean(
        axis=(2, 4, 6)
    )
    coarse_visc = visc_ext.reshape(half_rows + 2, 2, half_cols + 2, 2, half_levels + 2, 2).mean(
        axis=(1, 3, 5)
    )
    coarse_coefs = face_terms(coarse_visc, 0.125)
    coarse_diag = diagonal_of(coarse_coefs)
    coarse_error = RELAX * coarse_rhs / coarse_diag
    for turn_index in range(COARSE - 1):
        coarse_grown = with_halo(coarse_error, (("lat", 1), ("lon", 2)), 1)
        coarse_pad = jnp.pad(coarse_grown, ((0, 0), (0, 0), (0, 0), (1, 1)))
        coarse_error = (
            coarse_error
            + RELAX
            * (coarse_rhs - (coarse_diag * coarse_error - neighbour_sum(coarse_pad, coarse_coefs)))
            / coarse_diag
        )
    correction = jnp.repeat(jnp.repeat(jnp.repeat(coarse_error, 2, axis=1), 2, axis=2), 2, axis=3)
    new_field = smoothed + correction
    return (new_field[None], residual_field[None])


def solution(mesh):
    placed = (
        P("patch", None, "lat", "lon", None),
        P("patch", None, "lat", "lon", None),
        P("patch", "lat", "lon", None),
        P("patch", None),
        P("patch", "lat", "lon"),
        P("patch", "lat", "lon"),
        P("patch", "lat", None, "lon"),
    )
    return jax.shard_map(
        per_device,
        mesh=mesh,
        in_specs=placed,
        out_specs=(P("patch", None, "lat", "lon", None), P("patch", None, "lat", "lon", None)),
        check_vma=False,
    )
```

profile of v0, /device:TPU:6, one launch (start us, length us, event | category | flops | bytes accessed | tf_op | source)
XLA Modules:
  0.0 1015.0 jit_solution(3838266500594718935)
XLA Ops:
  8.3 3.5 collective-permute-start.4
  13.2 4.2 collective-permute-done.5
  20.9 4.5 collective-permute-done.7
  35.1 3.5 collective-permute-start
  43.9 677.3 %all-gather = f32[256,3,4]{2,1,0:T(4,128)S(1)} all-gather(f32[1,3,4]{2,1,0:T(4,128)S(1)} %bitcast.274), channel_id=1, replica_groups=mesh['patch'=2,'lat'=8,'lon'=32] {'lat','lon'}, dimensions={0}, use_global_device_ids=true | all-gather | bytes 12336 | tf_op jit(solution)/shard_map/all_gather | solution.py:148
  724.7 3.6 collective-permute-start.2
  728.2 5.2 collective-permute-start.3
  740.1 8.1 copy.123
  764.4 4.2 collective-permute-done.11
  768.7 4.4 collective-permute-start.12
  773.0 3.8 collective-permute-start.13
  776.9 4.1 collective-permute-done.13
  785.1 9.4 collective-permute-done.15
  796.5 3.9 collective-permute-start.17
  800.5 4.0 collective-permute-done.17
  805.6 5.1 collective-permute-start.18
  812.1 4.2 collective-permute-done.19
  818.3 4.1 collective-permute-start.21
  822.6 4.8 reshape.1395
  827.3 4.6 reduce_sum.19
  833.0 3.9 collective-permute-start.22
  838.4 4.2 collective-permute-done.23
  842.6 4.0 collective-permute-start.24
  848.7 5.9 collective-permute-done.25
  855.6 14.0 %reshape.1394 = f32[3,8,2,4,2,64,2]{6,5,4,3,2,1,0:T(8,128)} reshape(f32[3,16,8,128]{3,2,1,0:T(8,128)S(1)} %copy.142) | data formatting | bytes 393216 | tf_op jit(solution)/shard_map/reshape | solution.py:234
  869.6 5.5 reduce_sum.18
  879.7 4.2 collective-permute-done.27
  885.8 3.9 collective-permute-start.29
  889.8 3.7 collective-permute-done.29
  893.9 3.1 collective-permute-start.30
  898.3 4.2 collective-permute-done.31
  904.5 3.9 collective-permute-start.33
  908.4 3.8 collective-permute-done.33
  917.0 4.2 collective-permute-done.35
  923.2 3.9 collective-permute-start.37
  927.1 3.8 collective-permute-done.37
  935.7 4.2 collective-permute-done.39
  941.9 3.9 collective-permute-start.41
  945.8 3.8 collective-permute-done.41
  954.4 4.2 collective-permute-done.43
  960.6 3.9 collective-permute-start.45
  964.5 3.8 collective-permute-done.45
  968.6 3.1 collective-permute-start.46
  973.1 4.2 collective-permute-done.47
  979.2 3.9 collective-permute-start.49
  983.2 3.8 collective-permute-done.49
  991.8 4.2 collective-permute-done.51
  997.9 3.9 collective-permute-start.53
  (260 shorter events, 109.5 us)
Async XLA Ops:
  7.2 732.9 %all-gather.3.cloned.1.call-start = ((), (), s32[]{:S(2)}) async-start(), calls=%async_computation | async-start | bytes 6316032 | tf_op jit(solution)/shard_map/all_gather | solution.py:147
  8.3 4.9 collective-permute-start.4
  11.8 5.6 collective-permute-start.5
  17.5 8.0 collective-permute-start.7
  32.3 11.4 %collective-permute-start.8 = (f32[3,4]{0,1:T(4,128)S(1)}, f32[3,4]{0,1:T(4,128)S(1)}, u32[]{:S(2)}, u32[]{:S(2)}) collective-permute-start(f32[3,4]{0,1:T(4,128)S(1)} %bitcast.275), channel_id=1, source_target_pairs={{0,256},{256,0},{1,257},{257,1},{2,258},{258,2},{3,259},{259,3},{4... | collective-permute-start | bytes 152 | tf_op jit(solution)/shard_map/ppermute | solution.py:27
  35.1 689.5 %collective-permute-start = (f32[2,8,128]{2,1,0:T(8,128)S(1)}, f32[2,8,128]{2,1,0:T(8,128)S(1)}, u32[]{:S(2)}, u32[]{:S(2)}) collective-permute-start(f32[2,8,128]{2,1,0:T(8,128)S(1)} %get-tuple-element.390), channel_id=1, source_target_pairs={{0,32},{32,64},{64,96},{96,128},{128,160},{160,192},{192,224},{1,3... | collective-permute-start | bytes 24584 | tf_op jit(solution)/shard_map/ppermute | solution.py:18
  38.6 686.0 %collective-permute-start.1 = (f32[2,8,128]{2,1,0:T(8,128)S(1)}, f32[2,8,128]{2,1,0:T(8,128)S(1)}, u32[]{:S(2)}, u32[]{:S(2)}) collective-permute-start(f32[2,8,128]{2,1,0:T(8,128)S(1)} %get-tuple-element.391), channel_id=1, source_target_pairs={{32,0},{64,32},{96,64},{128,96},{160,128},{192,160},{224,192},{33,... | collective-permute-start | bytes 24584 | tf_op jit(solution)/shard_map/ppermute | solution.py:19
  724.7 11.8 %collective-permute-start.2 = (f32[20,2,128]{2,1,0:T(2,128)S(1)}, f32[20,2,128]{2,1,0:T(2,128)S(1)}, u32[]{:S(2)}, u32[]{:S(2)}) collective-permute-start(f32[20,2,128]{2,1,0:T(2,128)S(1)} %get-tuple-element.388), channel_id=1, source_target_pairs={{0,1},{1,2},{2,3},{3,4},{4,5},{5,6},{6,7},{7,8},{8,9},{9,10},{10,1... | collective-permute-start | bytes 61448 | tf_op jit(solution)/shard_map/ppermute | solution.py:18
  728.2 8.2 collective-permute-start.3
  733.7 6.3 collective-permute-start.6
  763.0 5.6 collective-permute-start.11
  768.7 8.2 collective-permute-start.12
  773.0 8.0 collective-permute-start.13
  783.7 10.9 %collective-permute-start.15 = (f32[3,1,8,128]{3,0,2,1:T(4,128)S(1)}, f32[3,1,8,128]{3,0,2,1:T(4,128)S(1)}, u32[]{:S(2)}, u32[]{:S(2)}) collective-permute-start(f32[3,1,8,128]{3,0,2,1:T(4,128)S(1)} %get-tuple-element.368), channel_id=1, source_target_pairs={{32,0},{64,32},{96,64},{128,96},{160,128},{192,160},{224,192},{33,... | collective-permute-start | bytes 36872 | tf_op jit(solution)/shard_map/ppermute | solution.py:19
  794.6 5.9 collective-permute-start.16
  796.5 8.0 collective-permute-start.17
  805.6 6.6 collective-permute-start.18
  810.7 5.6 collective-permute-start.19
  816.3 15.6 %collective-permute-start.20 = (f32[3,18,1,128]{3,0,2,1:T(4,128)S(1)}, f32[3,18,1,128]{3,0,2,1:T(4,128)S(1)}, u32[]{:S(2)}, u32[]{:S(2)}) collective-permute-start(f32[3,18,1,128]{3,0,2,1:T(4,128)S(1)} %get-tuple-element.355), channel_id=1, source_target_pairs={{0,1},{1,2},{2,3},{3,4},{4,5},{5,6},{6,7},{7,8},{8,9},{9,10},{10,1... | collective-permute-start | bytes 82952 | tf_op jit(solution)/shard_map/ppermute | solution.py:18
  818.3 13.7 %collective-permute-start.21 = (f32[3,18,1,128]{3,0,2,1:T(4,128)S(1)}, f32[3,18,1,128]{3,0,2,1:T(4,128)S(1)}, u32[]{:S(2)}, u32[]{:S(2)}) collective-permute-start(f32[3,18,1,128]{3,0,2,1:T(4,128)S(1)} %get-tuple-element.356), channel_id=1, source_target_pairs={{1,0},{2,1},{3,2},{4,3},{5,4},{6,5},{7,6},{8,7},{9,8},{10,9},{11,1... | collective-permute-start | bytes 82952 | tf_op jit(solution)/shard_map/ppermute | solution.py:19
  833.0 5.4 collective-permute-start.22
  837.0 5.6 collective-permute-start.23
  842.6 6.1 collective-permute-start.24
  846.7 8.0 collective-permute-start.25
  878.3 5.5 collective-permute-start.27
  883.9 5.9 collective-permute-start.28
  885.8 7.7 collective-permute-start.29
  893.9 4.5 collective-permute-start.30
  897.0 5.5 collective-permute-start.31
  902.6 5.9 collective-permute-start.32
  904.5 7.7 collective-permute-start.33
  912.6 4.5 collective-permute-start.34
  915.7 5.5 collective-permute-start.35
  921.3 5.9 collective-permute-start.36
  923.2 7.7 collective-permute-start.37
  931.2 4.5 collective-permute-start.38
  934.4 5.5 collective-permute-start.39
  939.9 5.9 collective-permute-start.40
  941.9 7.7 collective-permute-start.41
  953.1 5.5 collective-permute-start.43
  958.6 5.9 collective-permute-start.44
  960.6 7.7 collective-permute-start.45
  971.8 5.5 collective-permute-start.47
  977.3 5.9 collective-permute-start.48
  979.2 7.7 collective-permute-start.49
  990.4 5.5 collective-permute-start.51
  996.0 6.6 collective-permute-start.52
  997.9 7.7 collective-permute-start.53
  (11 other events, 799.0 us)
Sparse Core Ops, SparseCore 0:
  31.7 133.1 all-gather.2
where the time goes:
time: 1020 us
  blocking collectives  677 us (66%)
  starting transfers between devices  143 us (14%)
  waiting for transfers between devices  103 us (10%)
  local copies, waits for them, and re-layouts  55 us (5%)
  other arithmetic  21 us (2%)
  between operations  15.5 us (2%)
    all_gather x1, blocking collectives, per_device(): lax.all_gather(partner_weights, ('lat', 'lon'), axis=0, tiled=True)  677 us
    ppermute x26, waiting for transfers between devices, with_halo(): after = lax.ppermute(first, axis, down)  100 us
    ppermute x26, starting transfers between devices, with_halo(): before = lax.ppermute(last, axis, up)  72.8 us
    ppermute x26, starting transfers between devices, with_halo(): after = lax.ppermute(first, axis, down)  66 us
  transfers between devices with their start and end apart: 55, of which 30 were waited for; matrix products, arithmetic and copies ran while one was open for 2% of the time, Pallas kernels for 0%

commit v1 on v0

--- a/solution.py
+++ b/solution.py
@@ -145,7 +145,12 @@
         (jnp.zeros((3, rim_slot.shape[0], levels), jnp.float32) for rim_slot in rim_slots)
     )
     piece_corners = lax.all_gather(partner_corners, ("lat", "lon"), axis=0, tiled=True)
-    piece_weights = lax.all_gather(partner_weights, ("lat", "lon"), axis=0, tiled=True)
+    piece_weights = jnp.concatenate(
+        lax.all_to_all(
+            jnp.stack([partner_weights] * lax.axis_size(("lat", "lon"))), ("lat", "lon"), 0, 0
+        ),
+        axis=0,
+    )
     count_here = piece_corners.shape[0]
     outcome = []
     for rim_index in range(4):

time: 1020 us -> 458 us (0.45)
  the two profiles are of different devices: /device:TPU:6 before, /device:TPU:198 now
where the time goes in v1:
time: 458 us; the launch traced here: 456 us
  waiting for transfers between devices  193 us (42%)
  starting transfers between devices  169 us (37%)
  local copies, waits for them, and re-layouts  57.4 us (13%)
  other arithmetic  21 us (5%)
  between operations  15.5 us (3%)
    ppermute x26, waiting for transfers between devices, with_halo(): after = lax.ppermute(first, axis, down)  110 us
    ppermute x26, starting transfers between devices, with_halo(): before = lax.ppermute(last, axis, up)  84.9 us
    all_gather x1, waiting for transfers between devices, per_device(): lax.all_gather(partner_corners, ('lat', 'lon'), axis=0, tiled=True)  75.8 us
    ppermute x26, starting transfers between devices, with_halo(): after = lax.ppermute(first, axis, down)  60.8 us
    all_to_all x1, starting transfers between devices, per_device(): lax.all_to_all(jnp.stack([partner_weights] * lax.axis_size(('lat', 'lon')...  19.1 us
    reshape x1, local copies, waits for them, and re-layouts, per_device(): residual_field.reshape(3, half_rows, 2, half_cols, 2, half_levels, 2)  14 us
    gather x4, local copies, waits for them, and re-layouts, per_device(): jnp.take(piece_corners, safe_ids, axis=0)  11.8 us
  transfers between devices with their start and end apart: 56, of which 31 were waited for; matrix products, arithmetic and copies ran while one was open for 5% of the time, Pallas kernels for 0%

profile of v1, /device:TPU:198, one launch (start us, length us, event | category | flops | bytes accessed | tf_op | source)
XLA Modules:
  0.0 455.6 jit_solution(16433542760269979192)
XLA Ops:
  8.3 3.5 collective-permute-start.4
  13.2 4.2 collective-permute-done.5
  20.9 5.7 %collective-permute-done.7 = f32[3,18,1,128]{3,0,2,1:T(4,128)S(1)} collective-permute-done((f32[3,18,1,128]{3,0,2,1:T(4,128)S(1)}, f32[3,18,1,128]{3,0,2,1:T(4,128)S(1)}, u32[]{:S(2)}, u32[]{:S(2)}) %collective-permute-start.7) | collective-permute-done | bytes 27680 | tf_op jit(solution)/shard_map/ppermute | solution.py:19
  36.4 3.5 collective-permute-start
  45.9 19.1 %all-to-all-start = ((f32[256,3,4]{1,2,0:T(4,128)}), f32[256,3,4]{1,2,0:T(4,128)S(1)}, u32[]{:S(2)}, u32[]{:S(2)}) async-start(f32[256,3,4]{1,2,0:T(4,128)} %stack.12), calls=%async_computation | async-start | bytes 1048576 | tf_op jit(solution)/shard_map/all_to_all | solution.py:149
  65.0 4.6 %collective-permute-start.2 = (f32[20,2,128]{2,1,0:T(2,128)S(1)}, f32[20,2,128]{2,1,0:T(2,128)S(1)}, u32[]{:S(2)}, u32[]{:S(2)}) collective-permute-start(f32[20,2,128]{2,1,0:T(2,128)S(1)} %get-tuple-element.388), channel_id=1, source_target_pairs={{0,1},{1,2},{2,3},{3,4},{4,5},{5,6},{6,7},{7,8},{8,9},{9,10},{10,1... | collective-permute-start | bytes 61448 | tf_op jit(solution)/shard_map/ppermute | solution.py:18
  71.5 7.4 %collective-permute-start.6 = (f32[3,18,1,128]{3,0,2,1:T(4,128)S(1)}, f32[3,18,1,128]{3,0,2,1:T(4,128)S(1)}, u32[]{:S(2)}, u32[]{:S(2)}) collective-permute-start(f32[3,18,1,128]{3,0,2,1:T(4,128)S(1)} %get-tuple-element.361), channel_id=1, source_target_pairs={{0,1},{1,2},{2,3},{3,4},{4,5},{5,6},{6,7},{7,8},{8,9},{9,10},{10,1... | collective-permute-start | bytes 82952 | tf_op jit(solution)/shard_map/ppermute | solution.py:18
  79.0 5.0 %all-to-all-done = f32[256,3,4]{1,2,0:T(4,128)S(1)} async-done(((f32[256,3,4]{1,2,0:T(4,128)}), f32[256,3,4]{1,2,0:T(4,128)S(1)}, u32[]{:S(2)}, u32[]{:S(2)}) %all-to-all-start) | async-done | bytes 12320 | tf_op jit(solution)/shard_map/all_to_all | solution.py:149
  91.8 75.8 %all-gather.2.cloned.1.call-done = f32[768,4,3,128]{3,2,0,1:T(4,128)} async-done(((f32[3,4,3,128]{3,2,0,1:T(4,128)}), f32[768,4,3,128]{3,2,0,1:T(4,128)}) %all-gather.2.cloned.1.call-update) | async-done | bytes 4718608 | tf_op jit(solution)/shard_map/all_gather | solution.py:147
  167.5 8.0 %copy.117 = f32[768,4,3,128]{3,1,2,0:T(4,128)} copy(f32[768,4,3,128]{3,2,0,1:T(4,128)} %all-gather.2.cloned.1.call-done) | data formatting | bytes 9437184 | tf_op jit(solution)/shard_map/all_gather | solution.py:147
  192.8 4.2 collective-permute-done.11
  197.1 7.9 %collective-permute-start.12 = (f32[3,18,1,128]{3,0,2,1:T(4,128)S(1)}, f32[3,18,1,128]{3,0,2,1:T(4,128)S(1)}, u32[]{:S(2)}, u32[]{:S(2)}) collective-permute-start(f32[3,18,1,128]{3,0,2,1:T(4,128)S(1)} %get-tuple-element.359), channel_id=1, source_target_pairs={{0,1},{1,2},{2,3},{3,4},{4,5},{5,6},{6,7},{7,8},{8,9},{9,10},{10,1... | collective-permute-start | bytes 82952 | tf_op jit(solution)/shard_map/ppermute | solution.py:18
  206.9 7.2 %collective-permute-done.13 = f32[3,18,1,128]{3,0,2,1:T(4,128)S(1)} collective-permute-done((f32[3,18,1,128]{3,0,2,1:T(4,128)S(1)}, f32[3,18,1,128]{3,0,2,1:T(4,128)S(1)}, u32[]{:S(2)}, u32[]{:S(2)}) %collective-permute-start.13) | collective-permute-done | bytes 27680 | tf_op jit(solution)/shard_map/ppermute | solution.py:19
  220.0 4.2 collective-permute-done.15
  226.2 3.9 collective-permute-start.17
  230.1 5.2 %collective-permute-done.17 = f32[3,18,1,128]{3,0,2,1:T(4,128)S(1)} collective-permute-done((f32[3,18,1,128]{3,0,2,1:T(4,128)S(1)}, f32[3,18,1,128]{3,0,2,1:T(4,128)S(1)}, u32[]{:S(2)}, u32[]{:S(2)}) %collective-permute-start.17) | collective-permute-done | bytes 27680 | tf_op jit(solution)/shard_map/ppermute | solution.py:19
  240.9 4.2 collective-permute-done.19
  247.0 4.1 collective-permute-start.21
  251.4 4.7 %reshape.1401 = f32[10,2,6,2,66,2]{5,4,1,0,3,2:T(8,128)} reshape(f32[20,12,132]{2,0,1:T(8,128)S(1)} %pad_maximum_fusion.8) | data formatting | bytes 253440 | tf_op jit(solution)/shard_map/reshape | solution.py:242
  256.1 4.6 %reduce_sum.19 = f32[10,6,66]{2,0,1:T(8,128)S(1)} reduce(f32[10,2,6,2,66,2]{5,4,1,0,3,2:T(8,128)} %reshape.1401, f32[]{:T(128)} %constant.689.clone.1), dimensions={1,3,5}, to_apply=%region_1.8 | reduce | flops 27720 | bytes 142564 | tf_op jit(solution)/shard_map/reduce_sum | solution.py:242
  261.8 3.9 collective-permute-start.22
  267.2 4.2 collective-permute-done.23
  271.4 5.2 %collective-permute-start.24 = (f32[3,18,1,128]{3,0,2,1:T(4,128)S(1)}, f32[3,18,1,128]{3,0,2,1:T(4,128)S(1)}, u32[]{:S(2)}, u32[]{:S(2)}) collective-permute-start(f32[3,18,1,128]{3,0,2,1:T(4,128)S(1)} %get-tuple-element.353), channel_id=1, source_target_pairs={{0,1},{1,2},{2,3},{3,4},{4,5},{5,6},{6,7},{7,8},{8,9},{9,10},{10,1... | collective-permute-start | bytes 82952 | tf_op jit(solution)/shard_map/ppermute | solution.py:18
  278.7 7.1 %collective-permute-done.25 = f32[3,18,1,128]{3,0,2,1:T(4,128)S(1)} collective-permute-done((f32[3,18,1,128]{3,0,2,1:T(4,128)S(1)}, f32[3,18,1,128]{3,0,2,1:T(4,128)S(1)}, u32[]{:S(2)}, u32[]{:S(2)}) %collective-permute-start.25) | collective-permute-done | bytes 27680 | tf_op jit(solution)/shard_map/ppermute | solution.py:19
  286.9 14.0 %reshape.1400 = f32[3,8,2,4,2,64,2]{6,5,4,3,2,1,0:T(8,128)} reshape(f32[3,16,8,128]{3,2,1,0:T(8,128)S(1)} %copy.136) | data formatting | bytes 393216 | tf_op jit(solution)/shard_map/reshape | solution.py:239
  300.8 5.5 %reduce_sum.18 = f32[3,8,4,64]{3,2,1,0:T(4,128)S(1)} reduce(f32[3,8,2,4,2,64,2]{6,5,4,3,2,1,0:T(8,128)} %reshape.1400, f32[]{:T(128)} %constant.689.clone.1), dimensions={2,4,6}, to_apply=%region_0.7 | reduce | flops 43008 | bytes 221188 | tf_op jit(solution)/shard_map/reduce_sum | solution.py:239
  311.0 4.2 collective-permute-done.27
  317.1 3.9 collective-permute-start.29
  321.2 4.9 %collective-permute-done.29 = f32[3,10,1,64]{3,2,1,0:T(1,128)S(1)} collective-permute-done((f32[3,10,1,64]{3,2,1,0:T(1,128)S(1)}, f32[3,10,1,64]{3,2,1,0:T(1,128)S(1)}, u32[]{:S(2)}, u32[]{:S(2)}) %collective-permute-start.29) | collective-permute-done | bytes 7712 | tf_op jit(solution)/shard_map/ppermute | solution.py:19
  326.4 4.0 collective-permute-start.30
  331.7 4.2 collective-permute-done.31
  337.9 3.9 collective-permute-start.33
  341.8 5.0 %collective-permute-done.33 = f32[3,10,1,64]{3,2,1,0:T(1,128)S(1)} collective-permute-done((f32[3,10,1,64]{3,2,1,0:T(1,128)S(1)}, f32[3,10,1,64]{3,2,1,0:T(1,128)S(1)}, u32[]{:S(2)}, u32[]{:S(2)}) %collective-permute-start.33) | collective-permute-done | bytes 7712 | tf_op jit(solution)/shard_map/ppermute | solution.py:19
  351.6 4.2 collective-permute-done.35
  357.7 3.9 collective-permute-start.37
  361.7 5.0 %collective-permute-done.37 = f32[3,10,1,64]{3,2,1,0:T(1,128)S(1)} collective-permute-done((f32[3,10,1,64]{3,2,1,0:T(1,128)S(1)}, f32[3,10,1,64]{3,2,1,0:T(1,128)S(1)}, u32[]{:S(2)}, u32[]{:S(2)}) %collective-permute-start.37) | collective-permute-done | bytes 7712 | tf_op jit(solution)/shard_map/ppermute | solution.py:19
  371.5 4.2 collective-permute-done.39
  377.6 3.9 collective-permute-start.41
  381.6 5.0 %collective-permute-done.41 = f32[3,10,1,64]{3,2,1,0:T(1,128)S(1)} collective-permute-done((f32[3,10,1,64]{3,2,1,0:T(1,128)S(1)}, f32[3,10,1,64]{3,2,1,0:T(1,128)S(1)}, u32[]{:S(2)}, u32[]{:S(2)}) %collective-permute-start.41) | collective-permute-done | bytes 7712 | tf_op jit(solution)/shard_map/ppermute | solution.py:19
  391.4 4.2 collective-permute-done.43
  397.5 3.9 collective-permute-start.45
  401.4 5.0 %collective-permute-done.45 = f32[3,10,1,64]{3,2,1,0:T(1,128)S(1)} collective-permute-done((f32[3,10,1,64]{3,2,1,0:T(1,128)S(1)}, f32[3,10,1,64]{3,2,1,0:T(1,128)S(1)}, u32[]{:S(2)}, u32[]{:S(2)}) %collective-permute-start.45) | collective-permute-done | bytes 7712 | tf_op jit(solution)/shard_map/ppermute | solution.py:19
  411.2 4.2 collective-permute-done.47
  417.4 3.9 collective-permute-start.49
  421.3 5.0 %collective-permute-done.49 = f32[3,10,1,64]{3,2,1,0:T(1,128)S(1)} collective-permute-done((f32[3,10,1,64]{3,2,1,0:T(1,128)S(1)}, f32[3,10,1,64]{3,2,1,0:T(1,128)S(1)}, u32[]{:S(2)}, u32[]{:S(2)}) %collective-permute-start.49) | collective-permute-done | bytes 7712 | tf_op jit(solution)/shard_map/ppermute | solution.py:19
  431.1 4.2 collective-permute-done.51
  437.3 3.9 collective-permute-start.53
  441.9 4.3 collective-permute-done.53
  (262 shorter events, 117.8 us)
Async XLA Ops:
  7.2 160.3 %all-gather.2.cloned.1.call-start = ((), (), s32[]{:S(2)}) async-start(), calls=%async_computation.1 | async-start | bytes 6316032 | tf_op jit(solution)/shard_map/all_gather | solution.py:147
  8.3 4.9 %collective-permute-start.4 = (f32[3,1,8,128]{3,0,2,1:T(4,128)S(1)}, f32[3,1,8,128]{3,0,2,1:T(4,128)S(1)}, u32[]{:S(2)}, u32[]{:S(2)}) collective-permute-start(f32[3,1,8,128]{3,0,2,1:T(4,128)S(1)} %get-tuple-element.371), channel_id=1, source_target_pairs={{0,32},{32,64},{64,96},{96,128},{128,160},{160,192},{192,224},{1,3... | collective-permute-start | bytes 36872 | tf_op jit(solution)/shard_map/ppermute | solution.py:18
  11.8 5.6 %collective-permute-start.5 = (f32[3,1,8,128]{3,0,2,1:T(4,128)S(1)}, f32[3,1,8,128]{3,0,2,1:T(4,128)S(1)}, u32[]{:S(2)}, u32[]{:S(2)}) collective-permute-start(f32[3,1,8,128]{3,0,2,1:T(4,128)S(1)} %get-tuple-element.372), channel_id=1, source_target_pairs={{32,0},{64,32},{96,64},{128,96},{160,128},{192,160},{224,192},{33,... | collective-permute-start | bytes 36872 | tf_op jit(solution)/shard_map/ppermute | solution.py:19
  17.5 9.2 %collective-permute-start.7 = (f32[3,18,1,128]{3,0,2,1:T(4,128)S(1)}, f32[3,18,1,128]{3,0,2,1:T(4,128)S(1)}, u32[]{:S(2)}, u32[]{:S(2)}) collective-permute-start(f32[3,18,1,128]{3,0,2,1:T(4,128)S(1)} %get-tuple-element.362), channel_id=1, source_target_pairs={{1,0},{2,1},{3,2},{4,3},{5,4},{6,5},{7,6},{8,7},{9,8},{10,9},{11,1... | collective-permute-start | bytes 82952 | tf_op jit(solution)/shard_map/ppermute | solution.py:19
  33.6 11.4 %collective-permute-start.8 = (f32[3,4]{0,1:T(4,128)S(1)}, f32[3,4]{0,1:T(4,128)S(1)}, u32[]{:S(2)}, u32[]{:S(2)}) collective-permute-start(f32[3,4]{0,1:T(4,128)S(1)} %bitcast.273), channel_id=1, source_target_pairs={{0,256},{256,0},{1,257},{257,1},{2,258},{258,2},{3,259},{259,3},{4... | collective-permute-start | bytes 152 | tf_op jit(solution)/shard_map/ppermute | solution.py:27
  36.4 28.6 %collective-permute-start = (f32[2,8,128]{2,1,0:T(8,128)S(1)}, f32[2,8,128]{2,1,0:T(8,128)S(1)}, u32[]{:S(2)}, u32[]{:S(2)}) collective-permute-start(f32[2,8,128]{2,1,0:T(8,128)S(1)} %get-tuple-element.390), channel_id=1, source_target_pairs={{0,32},{32,64},{64,96},{96,128},{128,160},{160,192},{192,224},{1,3... | collective-permute-start | bytes 24584 | tf_op jit(solution)/shard_map/ppermute | solution.py:18
  39.8 25.1 %collective-permute-start.1 = (f32[2,8,128]{2,1,0:T(8,128)S(1)}, f32[2,8,128]{2,1,0:T(8,128)S(1)}, u32[]{:S(2)}, u32[]{:S(2)}) collective-permute-start(f32[2,8,128]{2,1,0:T(8,128)S(1)} %get-tuple-element.391), channel_id=1, source_target_pairs={{32,0},{64,32},{96,64},{128,96},{160,128},{192,160},{224,192},{33,... | collective-permute-start | bytes 24584 | tf_op jit(solution)/shard_map/ppermute | solution.py:19
  45.9 38.1 %all-to-all-start = ((f32[256,3,4]{1,2,0:T(4,128)}), f32[256,3,4]{1,2,0:T(4,128)S(1)}, u32[]{:S(2)}, u32[]{:S(2)}) async-start(f32[256,3,4]{1,2,0:T(4,128)} %stack.12), calls=%async_computation | async-start | bytes 1048576 | tf_op jit(solution)/shard_map/all_to_all | solution.py:149
  65.0 24.3 %collective-permute-start.2 = (f32[20,2,128]{2,1,0:T(2,128)S(1)}, f32[20,2,128]{2,1,0:T(2,128)S(1)}, u32[]{:S(2)}, u32[]{:S(2)}) collective-permute-start(f32[20,2,128]{2,1,0:T(2,128)S(1)} %get-tuple-element.388), channel_id=1, source_target_pairs={{0,1},{1,2},{2,3},{3,4},{4,5},{5,6},{6,7},{7,8},{8,9},{9,10},{10,1... | collective-permute-start | bytes 61448 | tf_op jit(solution)/shard_map/ppermute | solution.py:18
  69.6 19.7 %collective-permute-start.3 = (f32[20,2,128]{2,1,0:T(2,128)S(1)}, f32[20,2,128]{2,1,0:T(2,128)S(1)}, u32[]{:S(2)}, u32[]{:S(2)}) collective-permute-start(f32[20,2,128]{2,1,0:T(2,128)S(1)} %get-tuple-element.389), channel_id=1, source_target_pairs={{1,0},{2,1},{3,2},{4,3},{5,4},{6,5},{7,6},{8,7},{9,8},{10,9},{11,1... | collective-permute-start | bytes 61448 | tf_op jit(solution)/shard_map/ppermute | solution.py:19
  71.5 20.1 %collective-permute-start.6 = (f32[3,18,1,128]{3,0,2,1:T(4,128)S(1)}, f32[3,18,1,128]{3,0,2,1:T(4,128)S(1)}, u32[]{:S(2)}, u32[]{:S(2)}) collective-permute-start(f32[3,18,1,128]{3,0,2,1:T(4,128)S(1)} %get-tuple-element.361), channel_id=1, source_target_pairs={{0,1},{1,2},{2,3},{3,4},{4,5},{5,6},{6,7},{7,8},{8,9},{9,10},{10,1... | collective-permute-start | bytes 82952 | tf_op jit(solution)/shard_map/ppermute | solution.py:18
  191.4 5.6 %collective-permute-start.11 = (f32[3,1,8,128]{3,0,2,1:T(4,128)S(1)}, f32[3,1,8,128]{3,0,2,1:T(4,128)S(1)}, u32[]{:S(2)}, u32[]{:S(2)}) collective-permute-start(f32[3,1,8,128]{3,0,2,1:T(4,128)S(1)} %get-tuple-element.370), channel_id=1, source_target_pairs={{32,0},{64,32},{96,64},{128,96},{160,128},{192,160},{224,192},{33,... | collective-permute-start | bytes 36872 | tf_op jit(solution)/shard_map/ppermute | solution.py:19
  197.1 9.8 %collective-permute-start.12 = (f32[3,18,1,128]{3,0,2,1:T(4,128)S(1)}, f32[3,18,1,128]{3,0,2,1:T(4,128)S(1)}, u32[]{:S(2)}, u32[]{:S(2)}) collective-permute-start(f32[3,18,1,128]{3,0,2,1:T(4,128)S(1)} %get-tuple-element.359), channel_id=1, source_target_pairs={{0,1},{1,2},{2,3},{3,4},{4,5},{5,6},{6,7},{7,8},{8,9},{9,10},{10,1... | collective-permute-start | bytes 82952 | tf_op jit(solution)/shard_map/ppermute | solution.py:18
  205.0 9.2 %collective-permute-start.13 = (f32[3,18,1,128]{3,0,2,1:T(4,128)S(1)}, f32[3,18,1,128]{3,0,2,1:T(4,128)S(1)}, u32[]{:S(2)}, u32[]{:S(2)}) collective-permute-start(f32[3,18,1,128]{3,0,2,1:T(4,128)S(1)} %get-tuple-element.360), channel_id=1, source_target_pairs={{1,0},{2,1},{3,2},{4,3},{5,4},{6,5},{7,6},{8,7},{9,8},{10,9},{11,1... | collective-permute-start | bytes 82952 | tf_op jit(solution)/shard_map/ppermute | solution.py:19
  215.2 4.8 %collective-permute-start.14 = (f32[3,1,8,128]{3,0,2,1:T(4,128)S(1)}, f32[3,1,8,128]{3,0,2,1:T(4,128)S(1)}, u32[]{:S(2)}, u32[]{:S(2)}) collective-permute-start(f32[3,1,8,128]{3,0,2,1:T(4,128)S(1)} %get-tuple-element.367), channel_id=1, source_target_pairs={{0,32},{32,64},{64,96},{96,128},{128,160},{160,192},{192,224},{1,3... | collective-permute-start | bytes 36872 | tf_op jit(solution)/shard_map/ppermute | solution.py:18
  218.6 5.6 %collective-permute-start.15 = (f32[3,1,8,128]{3,0,2,1:T(4,128)S(1)}, f32[3,1,8,128]{3,0,2,1:T(4,128)S(1)}, u32[]{:S(2)}, u32[]{:S(2)}) collective-permute-start(f32[3,1,8,128]{3,0,2,1:T(4,128)S(1)} %get-tuple-element.368), channel_id=1, source_target_pairs={{32,0},{64,32},{96,64},{128,96},{160,128},{192,160},{224,192},{33,... | collective-permute-start | bytes 36872 | tf_op jit(solution)/shard_map/ppermute | solution.py:19
  224.3 5.9 %collective-permute-start.16 = (f32[3,18,1,128]{3,0,2,1:T(4,128)S(1)}, f32[3,18,1,128]{3,0,2,1:T(4,128)S(1)}, u32[]{:S(2)}, u32[]{:S(2)}) collective-permute-start(f32[3,18,1,128]{3,0,2,1:T(4,128)S(1)} %get-tuple-element.357), channel_id=1, source_target_pairs={{0,1},{1,2},{2,3},{3,4},{4,5},{5,6},{6,7},{7,8},{8,9},{9,10},{10,1... | collective-permute-start | bytes 82952 | tf_op jit(solution)/shard_map/ppermute | solution.py:18
  226.2 9.2 %collective-permute-start.17 = (f32[3,18,1,128]{3,0,2,1:T(4,128)S(1)}, f32[3,18,1,128]{3,0,2,1:T(4,128)S(1)}, u32[]{:S(2)}, u32[]{:S(2)}) collective-permute-start(f32[3,18,1,128]{3,0,2,1:T(4,128)S(1)} %get-tuple-element.358), channel_id=1, source_target_pairs={{1,0},{2,1},{3,2},{4,3},{5,4},{6,5},{7,6},{8,7},{9,8},{10,9},{11,1... | collective-permute-start | bytes 82952 | tf_op jit(solution)/shard_map/ppermute | solution.py:19
  239.5 5.6 %collective-permute-start.19 = (f32[3,1,8,128]{3,0,2,1:T(4,128)S(1)}, f32[3,1,8,128]{3,0,2,1:T(4,128)S(1)}, u32[]{:S(2)}, u32[]{:S(2)}) collective-permute-start(f32[3,1,8,128]{3,0,2,1:T(4,128)S(1)} %get-tuple-element.366), channel_id=1, source_target_pairs={{32,0},{64,32},{96,64},{128,96},{160,128},{192,160},{224,192},{33,... | collective-permute-start | bytes 36872 | tf_op jit(solution)/shard_map/ppermute | solution.py:19
  245.1 15.6 %collective-permute-start.20 = (f32[3,18,1,128]{3,0,2,1:T(4,128)S(1)}, f32[3,18,1,128]{3,0,2,1:T(4,128)S(1)}, u32[]{:S(2)}, u32[]{:S(2)}) collective-permute-start(f32[3,18,1,128]{3,0,2,1:T(4,128)S(1)} %get-tuple-element.355), channel_id=1, source_target_pairs={{0,1},{1,2},{2,3},{3,4},{4,5},{5,6},{6,7},{7,8},{8,9},{9,10},{10,1... | collective-permute-start | bytes 82952 | tf_op jit(solution)/shard_map/ppermute | solution.py:18
  247.0 13.7 %collective-permute-start.21 = (f32[3,18,1,128]{3,0,2,1:T(4,128)S(1)}, f32[3,18,1,128]{3,0,2,1:T(4,128)S(1)}, u32[]{:S(2)}, u32[]{:S(2)}) collective-permute-start(f32[3,18,1,128]{3,0,2,1:T(4,128)S(1)} %get-tuple-element.356), channel_id=1, source_target_pairs={{1,0},{2,1},{3,2},{4,3},{5,4},{6,5},{7,6},{8,7},{9,8},{10,9},{11,1... | collective-permute-start | bytes 82952 | tf_op jit(solution)/shard_map/ppermute | solution.py:19
  261.8 5.4 %collective-permute-start.22 = (f32[3,1,8,128]{3,0,2,1:T(4,128)S(1)}, f32[3,1,8,128]{3,0,2,1:T(4,128)S(1)}, u32[]{:S(2)}, u32[]{:S(2)}) collective-permute-start(f32[3,1,8,128]{3,0,2,1:T(4,128)S(1)} %get-tuple-element.363), channel_id=1, source_target_pairs={{0,32},{32,64},{64,96},{96,128},{128,160},{160,192},{192,224},{1,3... | collective-permute-start | bytes 36872 | tf_op jit(solution)/shard_map/ppermute | solution.py:18
  265.7 5.6 %collective-permute-start.23 = (f32[3,1,8,128]{3,0,2,1:T(4,128)S(1)}, f32[3,1,8,128]{3,0,2,1:T(4,128)S(1)}, u32[]{:S(2)}, u32[]{:S(2)}) collective-permute-start(f32[3,1,8,128]{3,0,2,1:T(4,128)S(1)} %get-tuple-element.364), channel_id=1, source_target_pairs={{32,0},{64,32},{96,64},{128,96},{160,128},{192,160},{224,192},{33,... | collective-permute-start | bytes 36872 | tf_op jit(solution)/shard_map/ppermute | solution.py:19
  271.4 7.3 %collective-permute-start.24 = (f32[3,18,1,128]{3,0,2,1:T(4,128)S(1)}, f32[3,18,1,128]{3,0,2,1:T(4,128)S(1)}, u32[]{:S(2)}, u32[]{:S(2)}) collective-permute-start(f32[3,18,1,128]{3,0,2,1:T(4,128)S(1)} %get-tuple-element.353), channel_id=1, source_target_pairs={{0,1},{1,2},{2,3},{3,4},{4,5},{5,6},{6,7},{7,8},{8,9},{9,10},{10,1... | collective-permute-start | bytes 82952 | tf_op jit(solution)/shard_map/ppermute | solution.py:18
  276.7 9.2 %collective-permute-start.25 = (f32[3,18,1,128]{3,0,2,1:T(4,128)S(1)}, f32[3,18,1,128]{3,0,2,1:T(4,128)S(1)}, u32[]{:S(2)}, u32[]{:S(2)}) collective-permute-start(f32[3,18,1,128]{3,0,2,1:T(4,128)S(1)} %get-tuple-element.354), channel_id=1, source_target_pairs={{1,0},{2,1},{3,2},{4,3},{5,4},{6,5},{7,6},{8,7},{9,8},{10,9},{11,1... | collective-permute-start | bytes 82952 | tf_op jit(solution)/shard_map/ppermute | solution.py:19
  306.4 4.6 %collective-permute-start.26 = (f32[3,1,4,64]{3,2,1,0:T(4,128)S(1)}, f32[3,1,4,64]{3,2,1,0:T(4,128)S(1)}, u32[]{:S(2)}, u32[]{:S(2)}) collective-permute-start(f32[3,1,4,64]{3,2,1,0:T(4,128)S(1)} %get-tuple-element.418), channel_id=1, source_target_pairs={{0,32},{32,64},{64,96},{96,128},{128,160},{160,192},{192,224},{1,3... | collective-permute-start | bytes 9224 | tf_op jit(solution)/shard_map/ppermute | solution.py:18
  309.7 5.5 %collective-permute-start.27 = (f32[3,1,4,64]{3,2,1,0:T(4,128)S(1)}, f32[3,1,4,64]{3,2,1,0:T(4,128)S(1)}, u32[]{:S(2)}, u32[]{:S(2)}) collective-permute-start(f32[3,1,4,64]{3,2,1,0:T(4,128)S(1)} %get-tuple-element.419), channel_id=1, source_target_pairs={{32,0},{64,32},{96,64},{128,96},{160,128},{192,160},{224,192},{33,... | collective-permute-start | bytes 9224 | tf_op jit(solution)/shard_map/ppermute | solution.py:19
  315.2 5.9 %collective-permute-start.28 = (f32[3,10,1,64]{3,2,1,0:T(1,128)S(1)}, f32[3,10,1,64]{3,2,1,0:T(1,128)S(1)}, u32[]{:S(2)}, u32[]{:S(2)}) collective-permute-start(f32[3,10,1,64]{3,2,1,0:T(1,128)S(1)} %get-tuple-element.404), channel_id=1, source_target_pairs={{0,1},{1,2},{2,3},{3,4},{4,5},{5,6},{6,7},{7,8},{8,9},{9,10},{10,1... | collective-permute-start | bytes 23048 | tf_op jit(solution)/shard_map/ppermute | solution.py:18
  317.1 8.9 %collective-permute-start.29 = (f32[3,10,1,64]{3,2,1,0:T(1,128)S(1)}, f32[3,10,1,64]{3,2,1,0:T(1,128)S(1)}, u32[]{:S(2)}, u32[]{:S(2)}) collective-permute-start(f32[3,10,1,64]{3,2,1,0:T(1,128)S(1)} %get-tuple-element.405), channel_id=1, source_target_pairs={{1,0},{2,1},{3,2},{4,3},{5,4},{6,5},{7,6},{8,7},{9,8},{10,9},{11,1... | collective-permute-start | bytes 23048 | tf_op jit(solution)/shard_map/ppermute | solution.py:19
  326.4 5.3 %collective-permute-start.30 = (f32[3,1,4,64]{3,2,1,0:T(4,128)S(1)}, f32[3,1,4,64]{3,2,1,0:T(4,128)S(1)}, u32[]{:S(2)}, u32[]{:S(2)}) collective-permute-start(f32[3,1,4,64]{3,2,1,0:T(4,128)S(1)} %get-tuple-element.416), channel_id=1, source_target_pairs={{0,32},{32,64},{64,96},{96,128},{128,160},{160,192},{192,224},{1,3... | collective-permute-start | bytes 9224 | tf_op jit(solution)/shard_map/ppermute | solution.py:18
  330.4 5.5 %collective-permute-start.31 = (f32[3,1,4,64]{3,2,1,0:T(4,128)S(1)}, f32[3,1,4,64]{3,2,1,0:T(4,128)S(1)}, u32[]{:S(2)}, u32[]{:S(2)}) collective-permute-start(f32[3,1,4,64]{3,2,1,0:T(4,128)S(1)} %get-tuple-element.417), channel_id=1, source_target_pairs={{32,0},{64,32},{96,64},{128,96},{160,128},{192,160},{224,192},{33,... | collective-permute-start | bytes 9224 | tf_op jit(solution)/shard_map/ppermute | solution.py:19
  335.9 5.9 %collective-permute-start.32 = (f32[3,10,1,64]{3,2,1,0:T(1,128)S(1)}, f32[3,10,1,64]{3,2,1,0:T(1,128)S(1)}, u32[]{:S(2)}, u32[]{:S(2)}) collective-permute-start(f32[3,10,1,64]{3,2,1,0:T(1,128)S(1)} %get-tuple-element.402), channel_id=1, source_target_pairs={{0,1},{1,2},{2,3},{3,4},{4,5},{5,6},{6,7},{7,8},{8,9},{9,10},{10,1... | collective-permute-start | bytes 23048 | tf_op jit(solution)/shard_map/ppermute | solution.py:18
  337.9 8.9 %collective-permute-start.33 = (f32[3,10,1,64]{3,2,1,0:T(1,128)S(1)}, f32[3,10,1,64]{3,2,1,0:T(1,128)S(1)}, u32[]{:S(2)}, u32[]{:S(2)}) collective-permute-start(f32[3,10,1,64]{3,2,1,0:T(1,128)S(1)} %get-tuple-element.403), channel_id=1, source_target_pairs={{1,0},{2,1},{3,2},{4,3},{5,4},{6,5},{7,6},{8,7},{9,8},{10,9},{11,1... | collective-permute-start | bytes 23048 | tf_op jit(solution)/shard_map/ppermute | solution.py:19
  350.2 5.5 %collective-permute-start.35 = (f32[3,1,4,64]{3,2,1,0:T(4,128)S(1)}, f32[3,1,4,64]{3,2,1,0:T(4,128)S(1)}, u32[]{:S(2)}, u32[]{:S(2)}) collective-permute-start(f32[3,1,4,64]{3,2,1,0:T(4,128)S(1)} %get-tuple-element.415), channel_id=1, source_target_pairs={{32,0},{64,32},{96,64},{128,96},{160,128},{192,160},{224,192},{33,... | collective-permute-start | bytes 9224 | tf_op jit(solution)/shard_map/ppermute | solution.py:19
  355.8 5.9 %collective-permute-start.36 = (f32[3,10,1,64]{3,2,1,0:T(1,128)S(1)}, f32[3,10,1,64]{3,2,1,0:T(1,128)S(1)}, u32[]{:S(2)}, u32[]{:S(2)}) collective-permute-start(f32[3,10,1,64]{3,2,1,0:T(1,128)S(1)} %get-tuple-element.400), channel_id=1, source_target_pairs={{0,1},{1,2},{2,3},{3,4},{4,5},{5,6},{6,7},{7,8},{8,9},{9,10},{10,1... | collective-permute-start | bytes 23048 | tf_op jit(solution)/shard_map/ppermute | solution.py:18
  357.7 8.9 %collective-permute-start.37 = (f32[3,10,1,64]{3,2,1,0:T(1,128)S(1)}, f32[3,10,1,64]{3,2,1,0:T(1,128)S(1)}, u32[]{:S(2)}, u32[]{:S(2)}) collective-permute-start(f32[3,10,1,64]{3,2,1,0:T(1,128)S(1)} %get-tuple-element.401), channel_id=1, source_target_pairs={{1,0},{2,1},{3,2},{4,3},{5,4},{6,5},{7,6},{8,7},{9,8},{10,9},{11,1... | collective-permute-start | bytes 23048 | tf_op jit(solution)/shard_map/ppermute | solution.py:19
  370.1 5.5 %collective-permute-start.39 = (f32[3,1,4,64]{3,2,1,0:T(4,128)S(1)}, f32[3,1,4,64]{3,2,1,0:T(4,128)S(1)}, u32[]{:S(2)}, u32[]{:S(2)}) collective-permute-start(f32[3,1,4,64]{3,2,1,0:T(4,128)S(1)} %get-tuple-element.413), channel_id=1, source_target_pairs={{32,0},{64,32},{96,64},{128,96},{160,128},{192,160},{224,192},{33,... | collective-permute-start | bytes 9224 | tf_op jit(solution)/shard_map/ppermute | solution.py:19
  375.7 5.9 %collective-permute-start.40 = (f32[3,10,1,64]{3,2,1,0:T(1,128)S(1)}, f32[3,10,1,64]{3,2,1,0:T(1,128)S(1)}, u32[]{:S(2)}, u32[]{:S(2)}) collective-permute-start(f32[3,10,1,64]{3,2,1,0:T(1,128)S(1)} %get-tuple-element.398), channel_id=1, source_target_pairs={{0,1},{1,2},{2,3},{3,4},{4,5},{5,6},{6,7},{7,8},{8,9},{9,10},{10,1... | collective-permute-start | bytes 23048 | tf_op jit(solution)/shard_map/ppermute | solution.py:18
  377.6 8.9 %collective-permute-start.41 = (f32[3,10,1,64]{3,2,1,0:T(1,128)S(1)}, f32[3,10,1,64]{3,2,1,0:T(1,128)S(1)}, u32[]{:S(2)}, u32[]{:S(2)}) collective-permute-start(f32[3,10,1,64]{3,2,1,0:T(1,128)S(1)} %get-tuple-element.399), channel_id=1, source_target_pairs={{1,0},{2,1},{3,2},{4,3},{5,4},{6,5},{7,6},{8,7},{9,8},{10,9},{11,1... | collective-permute-start | bytes 23048 | tf_op jit(solution)/shard_map/ppermute | solution.py:19
  390.0 5.5 %collective-permute-start.43 = (f32[3,1,4,64]{3,2,1,0:T(4,128)S(1)}, f32[3,1,4,64]{3,2,1,0:T(4,128)S(1)}, u32[]{:S(2)}, u32[]{:S(2)}) collective-permute-start(f32[3,1,4,64]{3,2,1,0:T(4,128)S(1)} %get-tuple-element.411), channel_id=1, source_target_pairs={{32,0},{64,32},{96,64},{128,96},{160,128},{192,160},{224,192},{33,... | collective-permute-start | bytes 9224 | tf_op jit(solution)/shard_map/ppermute | solution.py:19
  395.6 5.9 %collective-permute-start.44 = (f32[3,10,1,64]{3,2,1,0:T(1,128)S(1)}, f32[3,10,1,64]{3,2,1,0:T(1,128)S(1)}, u32[]{:S(2)}, u32[]{:S(2)}) collective-permute-start(f32[3,10,1,64]{3,2,1,0:T(1,128)S(1)} %get-tuple-element.396), channel_id=1, source_target_pairs={{0,1},{1,2},{2,3},{3,4},{4,5},{5,6},{6,7},{7,8},{8,9},{9,10},{10,1... | collective-permute-start | bytes 23048 | tf_op jit(solution)/shard_map/ppermute | solution.py:18
  397.5 8.9 %collective-permute-start.45 = (f32[3,10,1,64]{3,2,1,0:T(1,128)S(1)}, f32[3,10,1,64]{3,2,1,0:T(1,128)S(1)}, u32[]{:S(2)}, u32[]{:S(2)}) collective-permute-start(f32[3,10,1,64]{3,2,1,0:T(1,128)S(1)} %get-tuple-element.397), channel_id=1, source_target_pairs={{1,0},{2,1},{3,2},{4,3},{5,4},{6,5},{7,6},{8,7},{9,8},{10,9},{11,1... | collective-permute-start | bytes 23048 | tf_op jit(solution)/shard_map/ppermute | solution.py:19
  409.9 5.5 %collective-permute-start.47 = (f32[3,1,4,64]{3,2,1,0:T(4,128)S(1)}, f32[3,1,4,64]{3,2,1,0:T(4,128)S(1)}, u32[]{:S(2)}, u32[]{:S(2)}) collective-permute-start(f32[3,1,4,64]{3,2,1,0:T(4,128)S(1)} %get-tuple-element.409), channel_id=1, source_target_pairs={{32,0},{64,32},{96,64},{128,96},{160,128},{192,160},{224,192},{33,... | collective-permute-start | bytes 9224 | tf_op jit(solution)/shard_map/ppermute | solution.py:19
  415.5 5.9 %collective-permute-start.48 = (f32[3,10,1,64]{3,2,1,0:T(1,128)S(1)}, f32[3,10,1,64]{3,2,1,0:T(1,128)S(1)}, u32[]{:S(2)}, u32[]{:S(2)}) collective-permute-start(f32[3,10,1,64]{3,2,1,0:T(1,128)S(1)} %get-tuple-element.394), channel_id=1, source_target_pairs={{0,1},{1,2},{2,3},{3,4},{4,5},{5,6},{6,7},{7,8},{8,9},{9,10},{10,1... | collective-permute-start | bytes 23048 | tf_op jit(solution)/shard_map/ppermute | solution.py:18
  417.4 8.9 %collective-permute-start.49 = (f32[3,10,1,64]{3,2,1,0:T(1,128)S(1)}, f32[3,10,1,64]{3,2,1,0:T(1,128)S(1)}, u32[]{:S(2)}, u32[]{:S(2)}) collective-permute-start(f32[3,10,1,64]{3,2,1,0:T(1,128)S(1)} %get-tuple-element.395), channel_id=1, source_target_pairs={{1,0},{2,1},{3,2},{4,3},{5,4},{6,5},{7,6},{8,7},{9,8},{10,9},{11,1... | collective-permute-start | bytes 23048 | tf_op jit(solution)/shard_map/ppermute | solution.py:19
  429.8 5.5 %collective-permute-start.51 = (f32[3,1,4,64]{3,2,1,0:T(4,128)S(1)}, f32[3,1,4,64]{3,2,1,0:T(4,128)S(1)}, u32[]{:S(2)}, u32[]{:S(2)}) collective-permute-start(f32[3,1,4,64]{3,2,1,0:T(4,128)S(1)} %get-tuple-element.407), channel_id=1, source_target_pairs={{32,0},{64,32},{96,64},{128,96},{160,128},{192,160},{224,192},{33,... | collective-permute-start | bytes 9224 | tf_op jit(solution)/shard_map/ppermute | solution.py:19
  435.4 6.6 %collective-permute-start.52 = (f32[3,10,1,64]{3,2,1,0:T(1,128)S(1)}, f32[3,10,1,64]{3,2,1,0:T(1,128)S(1)}, u32[]{:S(2)}, u32[]{:S(2)}) collective-permute-start(f32[3,10,1,64]{3,2,1,0:T(1,128)S(1)} %get-tuple-element.392), channel_id=1, source_target_pairs={{0,1},{1,2},{2,3},{3,4},{4,5},{5,6},{6,7},{7,8},{8,9},{9,10},{10,1... | collective-permute-start | bytes 23048 | tf_op jit(solution)/shard_map/ppermute | solution.py:18
  437.3 8.9 %collective-permute-start.53 = (f32[3,10,1,64]{3,2,1,0:T(1,128)S(1)}, f32[3,10,1,64]{3,2,1,0:T(1,128)S(1)}, u32[]{:S(2)}, u32[]{:S(2)}) collective-permute-start(f32[3,10,1,64]{3,2,1,0:T(1,128)S(1)} %get-tuple-element.393), channel_id=1, source_target_pairs={{1,0},{2,1},{3,2},{4,3},{5,4},{6,5},{7,6},{8,7},{9,8},{10,9},{11,1... | collective-permute-start | bytes 23048 | tf_op jit(solution)/shard_map/ppermute | solution.py:19
  (12 other events, 223.1 us)
Sparse Core Ops, SparseCore 0:
  32.9 134.5 all-gather.1
